TPU v7x, 512 devices: a whole 4x8x8 slice. The times are simulated.
512 devices in a mesh: row: 64 (over x, y, z_hi), col: 8 (over z_lo, core).
Axes of the slice: x: 4, y: 8, z: 8 (z_hi: 2, z_lo: 4; z = z_hi * 4 + z_lo), core: 2. Of those that a mesh axis runs over, the one named last changes fastest.
Arguments:
- features: float32 [16384, 512], P('row', 'col'), may hold values from -20 to 20
- adj_values: bfloat16 [256, 64, 4096], P('row', 'col'), may hold values from 0 to 0.0078125
- adj_cols: int32 [256, 64], P('row', 'col'), may hold values from 0 to 255, as said below
- adj_count: int32 [256], P('row'), may hold values from 16 to 64, as said below
Outputs:
- hop_one: float32 [16384, 512], P('row', 'col')
- hop_two: float32 [16384, 512], P('row', 'col')
Inputs may be any that keep to these rules, and one draw needn't show every extreme that they name: `adj_cols`: within one row block the column blocks of all 64 slots are distinct. `adj_count`: some row block has all 64 slots live.
All inputs are finite; a program needn't handle non-finite values.
Results may differ from a plain program's by a relative error of at most 0.0003.
Values may be sent and summed in bfloat16 or wider, within the bound.
A program may use at most 128 MiB of HBM per device.

v0:
```python
import jax
import jax.numpy as jnp
from jax import lax
from jax.sharding import PartitionSpec as P

BLK = 64


def masked_tiles(tile_all, adj_count):
    slot_total = tile_all.shape[1]
    slot_ids = jnp.arange(slot_total, dtype=jnp.int32)
    live_mask = (slot_ids[None, :] < adj_count[:, None]).astype(jnp.float32)
    weights = tile_all.astype(jnp.float32).reshape(tile_all.shape[0], slot_total, BLK, BLK)
    return weights * live_mask[:, :, None, None]


def propagate(slab, weights, col_all):
    feat_width = slab.shape[1]
    blocks = slab.reshape(-1, BLK, feat_width)

    def single(record):
        weight_set, col_ids = record
        picked = blocks[col_ids]
        return jnp.einsum("kij,kjf->if", weight_set, picked, precision=lax.Precision.HIGHEST)

    result = lax.map(single, (weights, col_all))
    return result.reshape(-1, feat_width)


def local(features, adj_values, adj_cols, adj_count):
    tile_all, col_all = (
        lax.all_gather(adj_values, "col", axis=1, tiled=True),
        lax.all_gather(adj_cols, "col", axis=1, tiled=True),
    )
    weights = masked_tiles(tile_all, adj_count)
    slab = lax.all_gather(features, "row", axis=0, tiled=True)
    hop_one = propagate(slab, weights, col_all)
    second_slab = lax.all_gather(hop_one, "row", axis=0, tiled=True)
    hop_two = propagate(second_slab, weights, col_all)
    return (hop_one, hop_two)


def solution(mesh):
    in_specs = (P("row", "col"), P("row", "col", None), P("row", "col"), P("row"))
    out_specs = (P("row", "col"), P("row", "col"))
    return jax.shard_map(local, mesh=mesh, in_specs=in_specs, out_specs=out_specs, check_vma=False)
```

profile of v0, /device:TPU:6, one launch (start us, length us, event | category | flops | bytes accessed | tf_op | source)
XLA Modules:
  0.0 467.0 jit_solution(14740028736777230822)
XLA Ops:
  8.7 15.2 %all-gather = s32[8,8,4]{1,2,0:T(4,128)S(1)} all-gather(s32[1,8,4]{1,2,0:T(4,128)} %bitcast.70), channel_id=1, replica_groups=mesh['row'=64,'col'=8] {'col'}, dimensions={0}, use_global_device_ids=true | all-gather | bytes 1152 | tf_op jit(solution)/shard_map/all_gather | solution.py:33
  24.7 31.9 %all-gather.5.cloned.1.call-done = bf16[4,64,4096]{2,1,0:T(8,128)(2,1)} async-done(((bf16[4,8,4096]{2,1,0:T(8,128)(2,1)}), bf16[4,64,4096]{2,1,0:T(8,128)(2,1)}) %all-gather.5.cloned.1.call-update) | async-done | bytes 2097168 | tf_op jit(solution)/shard_map/all_gather | solution.py:32
  56.5 7.0 %reshape.107 = f32[4,64,64,64]{3,2,1,0:T(8,128)} reshape(bf16[4,64,4096]{2,1,0:T(8,128)(2,1)} %all-gather.5.cloned.1.call-done) | data formatting | bytes 6291456 | tf_op jit(solution)/shard_map/reshape | solution.py:13
  63.5 7.2 %broadcast_multiply_fusion = f32[4,64,64,64]{3,2,1,0:T(8,128)} fusion(f32[4,64,64,64]{3,2,1,0:T(8,128)} %reshape.107, f32[4,64]{1,0:T(4,128)S(1)} %fusion.34), kind=kLoop, calls=%fused_computation.26 | loop fusion | flops 1048576 | bytes 8389632 | tf_op jit(solution)/shard_map/mul | solution.py:14
  70.8 9.0 %copy.25 = f32[4,64,64,64]{1,2,3,0:T(8,128)} copy(f32[4,64,64,64]{3,2,1,0:T(8,128)} %broadcast_multiply_fusion) | data formatting | bytes 8388608 | tf_op jit(solution)/shard_map/while | solution.py:26
  79.8 141.0 %all-gather.7.cloned.1.call-done = f32[16384,64]{0,1:T(8,128)} async-done(((f32[256,64]{0,1:T(8,128)}), f32[16384,64]{0,1:T(8,128)}) %all-gather.7.cloned.1.call-update) | async-done | bytes 4194320 | tf_op jit(solution)/shard_map/all_gather | solution.py:36
  220.8 6.9 %copy.24 = f32[16384,64]{1,0:T(8,128)} copy(f32[16384,64]{0,1:T(8,128)} %all-gather.7.cloned.1.call-done) | data formatting | bytes 8388608 | tf_op jit(solution)/shard_map/all_gather | solution.py:36
  227.6 35.2 %while.20 = (s32[]{:T(128)}, f32[4,64,64]{2,1,0:T(8,128)S(1)}, f32[4,64,64,64]{1,2,3,0:T(8,128)}, s32[4,64]{1,0:T(4,128)S(1)}, f32[256,64,64]{2,1,0:T(8,128)}, /*index=5*/s32[]{:T(128)}) while((s32[]{:T(128)}, f32[4,64,64]{2,1,0:T(8,128)S(1)}, f32[4,64,64,64]{1,2,3,0:T(8,128)}, s32[4,64]{1,0:T(4,128)S(1)}, f32[256,64,64]{2,1,0:T(8,128)}, ...), condition=%wide.region_1.2_spmd, body=%wide.region_0.1_spmd.sunk | while | flops 201327808 | bytes 6330441 | solution.py:26
  227.7 4.1 gather_fusion
  231.7 4.7 %fusion.46 = f32[4,64,64]{2,1,0:T(8,128)S(1)} fusion(f32[4,64,64]{2,1,0:T(8,128)S(1)} %get-tuple-element.172, s32[]{:T(128)} %get-tuple-element.171, f32[64,64,64]{2,1,0:T(8,128)S(1)} %gather_fusion, f32[4,64,64,64]{1,2,3,0:T(8,128)} %get-tuple-element.179), kind=kOutput, calls=%fused_computation.7.clone.1 | convolution fusion | flops 201326592 | bytes 4228096 | tf_op jit(solution)/shard_map/while/body/eval_jaxpr/kij,kjf->if/dot_general | solution.py:24
  240.5 4.7 %fusion.46 = f32[4,64,64]{2,1,0:T(8,128)S(1)} fusion(f32[4,64,64]{2,1,0:T(8,128)S(1)} %get-tuple-element.172, s32[]{:T(128)} %get-tuple-element.171, f32[64,64,64]{2,1,0:T(8,128)S(1)} %gather_fusion, f32[4,64,64,64]{1,2,3,0:T(8,128)} %get-tuple-element.179), kind=kOutput, calls=%fused_computation.7.clone.1 | convolution fusion | flops 201326592 | bytes 4228096 | tf_op jit(solution)/shard_map/while/body/eval_jaxpr/kij,kjf->if/dot_general | solution.py:24
  245.3 4.1 gather_fusion
  249.3 4.7 %fusion.46 = f32[4,64,64]{2,1,0:T(8,128)S(1)} fusion(f32[4,64,64]{2,1,0:T(8,128)S(1)} %get-tuple-element.172, s32[]{:T(128)} %get-tuple-element.171, f32[64,64,64]{2,1,0:T(8,128)S(1)} %gather_fusion, f32[4,64,64,64]{1,2,3,0:T(8,128)} %get-tuple-element.179), kind=kOutput, calls=%fused_computation.7.clone.1 | convolution fusion | flops 201326592 | bytes 4228096 | tf_op jit(solution)/shard_map/while/body/eval_jaxpr/kij,kjf->if/dot_general | solution.py:24
  254.1 4.1 gather_fusion
  258.1 4.7 %fusion.46 = f32[4,64,64]{2,1,0:T(8,128)S(1)} fusion(f32[4,64,64]{2,1,0:T(8,128)S(1)} %get-tuple-element.172, s32[]{:T(128)} %get-tuple-element.171, f32[64,64,64]{2,1,0:T(8,128)S(1)} %gather_fusion, f32[4,64,64,64]{1,2,3,0:T(8,128)} %get-tuple-element.179), kind=kOutput, calls=%fused_computation.7.clone.1 | convolution fusion | flops 201326592 | bytes 4228096 | tf_op jit(solution)/shard_map/while/body/eval_jaxpr/kij,kjf->if/dot_general | solution.py:24
  263.6 154.2 %all-gather.9.cloned.1.call-done = f32[16384,64]{0,1:T(8,128)} async-done(((f32[256,64]{0,1:T(8,128)}), f32[16384,64]{0,1:T(8,128)}) %all-gather.9.cloned.1.call-update) | async-done | bytes 4194320 | tf_op jit(solution)/shard_map/all_gather | solution.py:38
  417.8 6.9 %copy.31 = f32[16384,64]{1,0:T(8,128)} copy(f32[16384,64]{0,1:T(8,128)} %all-gather.9.cloned.1.call-done) | data formatting | bytes 8388608 | tf_op jit(solution)/shard_map/while | solution.py:26
  424.6 35.2 %while.21 = (s32[]{:T(128)}, f32[4,64,64]{2,1,0:T(8,128)S(1)}, f32[4,64,64,64]{1,2,3,0:T(8,128)}, s32[4,64]{1,0:T(4,128)S(1)}, f32[256,64,64]{2,1,0:T(8,128)}, /*index=5*/s32[]{:T(128)}) while((s32[]{:T(128)}, f32[4,64,64]{2,1,0:T(8,128)S(1)}, f32[4,64,64,64]{1,2,3,0:T(8,128)}, s32[4,64]{1,0:T(4,128)S(1)}, f32[256,64,64]{2,1,0:T(8,128)}, ...), condition=%wide.region_3.4_spmd, body=%wide.region_2.3_spmd.sunk | while | flops 201327808 | bytes 6330441 | solution.py:26
  424.7 4.1 gather_fusion.1
  428.7 4.7 %fusion.50 = f32[4,64,64]{2,1,0:T(8,128)S(1)} fusion(f32[4,64,64]{2,1,0:T(8,128)S(1)} %get-tuple-element.190, s32[]{:T(128)} %get-tuple-element.189, f32[64,64,64]{2,1,0:T(8,128)S(1)} %gather_fusion.1, f32[4,64,64,64]{1,2,3,0:T(8,128)} %get-tuple-element.197), kind=kOutput, calls=%fused_computation.19.clone.1 | convolution fusion | flops 201326592 | bytes 4228096 | tf_op jit(solution)/shard_map/while/body/eval_jaxpr/kij,kjf->if/dot_general | solution.py:24
  433.5 4.1 gather_fusion.1
  437.5 4.7 %fusion.50 = f32[4,64,64]{2,1,0:T(8,128)S(1)} fusion(f32[4,64,64]{2,1,0:T(8,128)S(1)} %get-tuple-element.190, s32[]{:T(128)} %get-tuple-element.189, f32[64,64,64]{2,1,0:T(8,128)S(1)} %gather_fusion.1, f32[4,64,64,64]{1,2,3,0:T(8,128)} %get-tuple-element.197), kind=kOutput, calls=%fused_computation.19.clone.1 | convolution fusion | flops 201326592 | bytes 4228096 | tf_op jit(solution)/shard_map/while/body/eval_jaxpr/kij,kjf->if/dot_general | solution.py:24
  446.3 4.7 %fusion.50 = f32[4,64,64]{2,1,0:T(8,128)S(1)} fusion(f32[4,64,64]{2,1,0:T(8,128)S(1)} %get-tuple-element.190, s32[]{:T(128)} %get-tuple-element.189, f32[64,64,64]{2,1,0:T(8,128)S(1)} %gather_fusion.1, f32[4,64,64,64]{1,2,3,0:T(8,128)} %get-tuple-element.197), kind=kOutput, calls=%fused_computation.19.clone.1 | convolution fusion | flops 201326592 | bytes 4228096 | tf_op jit(solution)/shard_map/while/body/eval_jaxpr/kij,kjf->if/dot_general | solution.py:24
  455.1 4.7 %fusion.50 = f32[4,64,64]{2,1,0:T(8,128)S(1)} fusion(f32[4,64,64]{2,1,0:T(8,128)S(1)} %get-tuple-element.190, s32[]{:T(128)} %get-tuple-element.189, f32[64,64,64]{2,1,0:T(8,128)S(1)} %gather_fusion.1, f32[4,64,64,64]{1,2,3,0:T(8,128)} %get-tuple-element.197), kind=kOutput, calls=%fused_computation.19.clone.1 | convolution fusion | flops 201326592 | bytes 4228096 | tf_op jit(solution)/shard_map/while/body/eval_jaxpr/kij,kjf->if/dot_general | solution.py:24
  (32 shorter events, 16.1 us)
Async XLA Ops:
  7.2 49.4 %all-gather.5.cloned.1.call-start = ((), (), s32[]{:S(2)}) async-start(), calls=%async_computation | async-start | bytes 2359296 | tf_op jit(solution)/shard_map/all_gather | solution.py:32
  7.9 212.9 %all-gather.7.cloned.1.call-start = ((), (), s32[]{:S(2)}) async-start(), calls=%async_computation.1 | async-start | bytes 4259840 | tf_op jit(solution)/shard_map/all_gather | solution.py:36
  8.6 409.1 %all-gather.9.cloned.1.call-start = ((), (), s32[]{:S(2)}) async-start(), calls=%async_computation.2 | async-start | bytes 4259840 | tf_op jit(solution)/shard_map/all_gather | solution.py:38
Sparse Core Ops, SparseCore 0:
  10.1 46.4 all-gather.4
  60.9 159.8 all-gather.6
  263.7 154.0 all-gather.8
where the time goes:
time: 468 us; the launch traced here: 467 us
  waiting for transfers between devices  328 us (70%)
  local copies, waits for them, and re-layouts  63.7 us (14%)
  matrix products  37.5 us (8%)
  blocking collectives  15.2 us (3%)
  between operations  13.8 us (3%)
  other arithmetic  8.08 us (2%)
    all_gather x1, waiting for transfers between devices, local(): second_slab = lax.all_gather(hop_one, 'row', axis=0, tiled=True)  154 us
    all_gather x1, waiting for transfers between devices, local(): slab = lax.all_gather(features, 'row', axis=0, tiled=True)  141 us
    dot_general x8, matrix products, single(): jnp.einsum('kij,kjf->if', weight_set, picked, precision=lax.Precision.HIG...  37.5 us
    gather x8, local copies, waits for them, and re-layouts, single(): picked = blocks[col_ids]  32.5 us
    all_gather x1, waiting for transfers between devices, local(): lax.all_gather(adj_values, 'col', axis=1, tiled=True)  31.9 us
    while x2, local copies, waits for them, and re-layouts, propagate(): result = lax.map(single, (weights, col_all))  15.9 us
    all_gather x1, blocking collectives, local(): lax.all_gather(adj_cols, 'col', axis=1, tiled=True)  15.2 us
  transfers between devices with their start and end apart: 3, of which 3 were waited for; matrix products, arithmetic and copies ran while one was open for 5% of the time, Pallas kernels for 0%

commit v1 on v0

v1 whole, which is shorter than its diff:
```python
import functools

import jax
import jax.numpy as jnp
from jax import lax
from jax.experimental import pallas as pl
from jax.experimental.pallas import tpu as pltpu
from jax.sharding import PartitionSpec as P

BLK = 64
NX, NY, NZ = 4, 8, 2
NC = 8
MESH = pl.DeviceIdType.MESH


def split_parts(x):
    hi = x.astype(jnp.bfloat16)
    lo = (x - hi.astype(jnp.float32)).astype(jnp.bfloat16)
    return jnp.concatenate([hi, lo], axis=-1)


def pack_kernel(x_ref, out_ref):
    out_ref[...] = split_parts(x_ref[...])


def pack(features):
    return pl.pallas_call(
        pack_kernel,
        out_shape=jax.ShapeDtypeStruct((256, 2 * BLK), jnp.bfloat16),
    )(features)


def ring_program():
    def stream(rel, half):
        tag = (rel, half)
        first, second = ("x", "y") if half == 0 else ("y", "x")
        size = {"x": NX, "y": NY}

        def phase(axis, whole):
            n = size[axis]
            steps = []
            for t in range(1, n // 2 + 1):
                sends = []
                for sign in (1, -1):
                    off = -sign * (t - 1)
                    slab = (off, whole) if axis == "x" else (whole, off)
                    sub = None if t < n // 2 else (0 if sign == 1 else 1)
                    sends.append(((tag, axis, t, sign), rel, half, slab, sub, axis, sign))
                steps.append(sends)
            return steps

        return phase(first, 0) + phase(second, None)

    program = []
    for rel in (0, 1):
        for half in (0, 1):
            steps = stream(rel, half)
            for t, sends in enumerate(steps):
                needs = [] if t == 0 else [s[0] for s in steps[t - 1]]
                if t == 0 and rel == 1:
                    needs = ["z"]
                program.append((t + 2 * rel, rel, half, needs, sends))
            program.append((len(steps) + 2 * rel, rel, half, [s[0] for s in steps[-1]], []))
    program.sort(key=lambda p: p[0])
    return program


def gather_kernel(with_adj, *refs):
    if with_adj:
        shard, tiles, cols, nodes, tiles_all, cols_all, send, recv, local, adj_send, adj_recv, adj_local = refs
    else:
        shard, nodes, send, recv, local = refs
    row = lax.axis_index("row")
    col = lax.axis_index("col")
    zh = lax.rem(row, NZ)
    y = lax.rem(row // NZ, NY)
    x = row // (NZ * NY)
    zl, core = col // 2, lax.rem(col, 2)

    def device(px, py, pz, c=None):
        return ((px * NY + py) * NZ + pz, col if c is None else c)

    def hop(axis, sign):
        if axis == "x":
            return device(lax.rem(x + sign + NX, NX), y, zh)
        return device(x, lax.rem(y + sign + NY, NY), zh)

    partners = [hop(a, s) for a in ("x", "y") for s in (1, -1)] + [device(x, y, 1 - zh)]
    if with_adj:
        others = [lax.rem(col + j, NC) for j in range(1, NC)]
        partners += [(row, c) for c in others]
    barrier = pltpu.get_barrier_semaphore()
    for p in partners:
        pl.semaphore_signal(barrier, inc=1, device_id=p, device_id_type=MESH)
    pl.semaphore_wait(barrier, len(partners))

    def slab_of(rel, half, slab, sub):
        ix = slice(None) if slab[0] is None else lax.rem(x + slab[0] + NX, NX)
        iy = slice(None) if slab[1] is None else lax.rem(y + slab[1] + NY, NY)
        iz = zh if rel == 0 else 1 - zh
        isub = slice(None) if sub is None else sub
        return nodes.at[ix, iy, iz, half, isub]

    order = {}
    flying = {}
    pending = []

    def remote(src, dst, sems, k, dev):
        c = pltpu.make_async_remote_copy(
            src_ref=src, dst_ref=dst, send_sem=sems[0].at[k], recv_sem=sems[1].at[k],
            device_id=dev, device_id_type=MESH)
        c.start()
        return c

    mine = nodes.at[x, y, zh]
    own = pltpu.make_async_copy(shard, mine, local)
    own.start()
    flying["z"] = remote(shard, mine, (send, recv), 0, device(x, y, 1 - zh))
    counter = 1
    adj = {}

    def issue(sends):
        nonlocal counter
        for key, rel, half, slab, sub, axis, sign in sends:
            dst = slab_of(rel, half, slab, sub)
            src = dst
            if rel == 0 and slab == (0, 0):
                src = shard.at[half] if sub is None else shard.at[half, sub]
            flying[key] = remote(src, dst, (send, recv), counter, hop(axis, sign))
            counter += 1

    waited_own = False
    waited = set()
    adj_started = False
    for slot, rel, half, needs, sends in ring_program():
        for key in needs:
            if key not in waited:
                flying[key].wait_recv()
                waited.add(key)
        if not waited_own and any(s[3] != (0, 0) for s in sends):
            own.wait()
            waited_own = True
        issue(sends)
        if with_adj and not adj_started and slot == 0 and half == 1:
            adj_started = True
            adj_own = [pltpu.make_async_copy(tiles, tiles_all.at[col], adj_local.at[0]),
                       pltpu.make_async_copy(cols, cols_all.at[col], adj_local.at[1])]
            for c in adj_own:
                c.start()
            across = [remote(tiles, tiles_all.at[col], (adj_send, adj_recv), j - 1,
                             (row, lax.rem(zl + j, 4) * 2 + core)) for j in range(1, 4)]
            twin = [remote(tiles, tiles_all.at[col], (adj_send, adj_recv), 3,
                           (row, zl * 2 + 1 - core))]
            ids = [remote(cols, cols_all.at[col], (adj_send, adj_recv), 7 + j,
                          (row, others[j])) for j in range(NC - 1)]
    if with_adj:
        for j in range(1, 4):
            across[j - 1].wait_recv()
            origin = lax.rem(zl + 4 - j, 4) * 2 + core
            piece = tiles_all.at[origin]
            twin.append(remote(piece, piece, (adj_send, adj_recv), 3 + j,
                               (row, zl * 2 + 1 - core)))
        for c in twin + ids:
            c.wait_recv()
        for c in across + twin + ids:
            c.wait_send()
        for c in adj_own:
            c.wait()
    for key in flying:
        flying[key].wait_send()


def gather(shard, tiles=None, cols=None, collective_id=0):
    with_adj = tiles is not None
    steps = 1 + sum(len(p[4]) for p in ring_program())
    out_shape = [jax.ShapeDtypeStruct((NX, NY, NZ, 2, 2, BLK, 2 * BLK), jnp.bfloat16)]
    args = [shard.reshape(2, 2, BLK, 2 * BLK)]
    scratch = [pltpu.SemaphoreType.DMA((steps,)), pltpu.SemaphoreType.DMA((steps,)),
               pltpu.SemaphoreType.DMA]
    if with_adj:
        out_shape += [jax.ShapeDtypeStruct((NC,) + tiles.shape, tiles.dtype),
                      jax.ShapeDtypeStruct((NC,) + cols.shape, cols.dtype)]
        args += [tiles, cols]
        scratch += [pltpu.SemaphoreType.DMA((14,)), pltpu.SemaphoreType.DMA((14,)),
                    pltpu.SemaphoreType.DMA((2,))]
    return pl.pallas_call(
        functools.partial(gather_kernel, with_adj),
        out_shape=out_shape,
        in_specs=[pl.BlockSpec(memory_space=pltpu.VMEM)] * len(args),
        out_specs=[pl.BlockSpec(memory_space=pl.ANY)] * len(out_shape),
        scratch_shapes=scratch,
        compiler_params=pltpu.CompilerParams(collective_id=collective_id, has_side_effects=True),
    )(*args)


def hop_kernel(packed, cols, tiles, nodes, out_ref, *packed_ref):
    for i in range(4):
        acc = jnp.zeros((BLK, 2 * BLK), jnp.float32)
        for j in range(NC):
            picked = jnp.concatenate([nodes[cols[j, i, s]] for s in range(8)], axis=0)
            acc += jnp.dot(tiles[j, i], picked, preferred_element_type=jnp.float32)
        total = acc[:, :BLK] + acc[:, BLK:]
        out_ref[pl.ds(i * BLK, BLK), :] = total
        if packed:
            packed_ref[0][pl.ds(i * BLK, BLK), :] = split_parts(total)


def hop(nodes, tiles, cols, packed):
    out_shape = [jax.ShapeDtypeStruct((256, BLK), jnp.float32)]
    if packed:
        out_shape.append(jax.ShapeDtypeStruct((256, 2 * BLK), jnp.bfloat16))
    return pl.pallas_call(
        functools.partial(hop_kernel, packed),
        out_shape=out_shape,
        in_specs=[pl.BlockSpec(memory_space=pltpu.SMEM)] + [pl.BlockSpec(memory_space=pltpu.VMEM)] * 2,
        out_specs=[pl.BlockSpec(memory_space=pltpu.VMEM)] * len(out_shape),
    )(cols, tiles, nodes.reshape(256, BLK, 2 * BLK))


def local(features, adj_values, adj_cols, adj_count):
    slots = lax.axis_index("col") * 8 + jnp.arange(8, dtype=jnp.int32)
    live = slots[None, :, None] < adj_count[:, None, None]
    tiles = jnp.where(live, adj_values, jnp.zeros_like(adj_values))
    tiles = tiles.reshape(4, 8, BLK, BLK).transpose(0, 2, 1, 3).reshape(4, BLK, 8 * BLK)
    cols = jnp.pad(adj_cols, ((0, 4), (0, 120)))
    nodes, tiles_all, cols_all = gather(pack(features), tiles, cols, collective_id=0)
    hop_one, shard = hop(nodes, tiles_all, cols_all, True)
    (second,) = gather(shard, collective_id=1)
    (hop_two,) = hop(second, tiles_all, cols_all, False)
    return hop_one, hop_two


def solution(mesh):
    in_specs = (P("row", "col"), P("row", "col", None), P("row", "col"), P("row"))
    out_specs = (P("row", "col"), P("row", "col"))
    return jax.shard_map(local, mesh=mesh, in_specs=in_specs, out_specs=out_specs, check_vma=False)
```

time: 468 us -> 134 us (0.29)
  the two profiles are of different devices: /device:TPU:6 before, /device:TPU:24 now
where the time goes in v1:
time: 134 us; the launch traced here: 133 us
  Pallas kernels  123 us (92%)
  local copies, waits for them, and re-layouts  8 us (6%)
  other arithmetic  1.77 us (1%)
    pallas_call x2, Pallas kernels, gather(): pl.pallas_call(functools.partial(gather_kernel, with_adj), out_shape=out_...  112 us
    pallas_call x2, Pallas kernels, hop(): pl.pallas_call(functools.partial(hop_kernel, packed), out_shape=out_shape...  8.94 us
    unnamed x3, local copies, waits for them, and re-layouts  4.8 us

profile of v1, /device:TPU:24, one launch (start us, length us, event | category | flops | bytes accessed | tf_op | source)
XLA Modules:
  0.0 133.3 jit_solution(4558646639294199107)
XLA Ops:
  0.6 0.7 broadcast_compare_fusion
  1.4 1.3 pad.4.refs_2_
  2.7 1.6 %copy.6.x_ref = f32[256,64]{1,0:T(8,128)} copy(f32[256,64]{0,1:T(8,128)} %param.4) | data formatting | bytes 131072 | tf_op args[0]
  4.2 1.6 %shard_map.59 = bf16[256,128]{1,0:T(8,128)(2,1)} custom-call(f32[256,64]{1,0:T(8,128)} %copy.6.x_ref), custom_call_target="tpu_custom_call" | custom-call | tf_op jit(solution)/shard_map/pallas_call | solution.py:27
  5.8 1.0 broadcast_select_fusion
  6.9 0.5 reshape.60
  7.4 0.3 copy.11
  7.8 1.0 reshape.61.refs_1_
  8.8 60.7 %shard_map.60 = (bf16[4,8,2,2,2,64,128]{6,5,4,3,2,1,0:T(8,128)(2,1)}, bf16[8,4,64,512]{3,2,1,0:T(8,128)(2,1)}, s32[8,8,128]{2,1,0:T(8,128)}) custom-call(bf16[2,2,64,128]{3,2,1,0:T(8,128)(2,1)} %bitcast.12, bf16[4,64,512]{2,1,0:T(8,128)(2,1)} %reshape.61.refs_1_, s32[8,128]{1,0:T(8,128)} %pad.4.refs_2_), custom_call_target="tpu_custom_call" | custom-call | tf_op jit(solution)/shard_map/pallas_call | solution.py:186
  69.6 4.5 %shard_map.61 = (f32[256,64]{1,0:T(8,128)}, bf16[256,128]{1,0:T(8,128)(2,1)}) custom-call(s32[8,8,128]{2,1,0:T(8,128)} %get-tuple-element.7.cols, bf16[8,4,64,512]{3,2,1,0:T(8,128)(2,1)} %get-tuple-element.8.tiles, bf16[256,64,128]{2,1,0:T(8,128)(2,1)} %bitcast.10), custom_call_target="tpu_custom_call" | custom-call | tf_op jit(solution)/shard_map/pallas_call | solution.py:212
  74.1 1.6 %copy.8 = f32[256,64]{0,1:T(8,128)} copy(f32[256,64]{1,0:T(8,128)} %get-tuple-element.12) | data formatting | bytes 131072
  75.7 51.6 %shard_map.62 = bf16[4,8,2,2,2,64,128]{6,5,4,3,2,1,0:T(8,128)(2,1)} custom-call(bf16[2,2,64,128]{3,2,1,0:T(8,128)(2,1)} %bitcast.13), custom_call_target="tpu_custom_call" | custom-call | tf_op jit(solution)/shard_map/pallas_call | solution.py:186
  127.3 4.4 %shard_map.63 = f32[256,64]{1,0:T(8,128)} custom-call(s32[8,8,128]{2,1,0:T(8,128)} %get-tuple-element.7.cols, bf16[8,4,64,512]{3,2,1,0:T(8,128)(2,1)} %get-tuple-element.8.tiles, bf16[256,64,128]{2,1,0:T(8,128)(2,1)} %bitcast.9), custom_call_target="tpu_custom_call" | custom-call | tf_op jit(solution)/shard_map/pallas_call | solution.py:212
  131.7 1.6 %copy.9 = f32[256,64]{0,1:T(8,128)} copy(f32[256,64]{1,0:T(8,128)} %shard_map.63) | data formatting | bytes 131072
  (1 shorter events, 0.0 us)

commit v2 on v1

--- a/solution.py
+++ b/solution.py
@@ -14,20 +14,59 @@
 
 
 def split_parts(x):
-    hi = x.astype(jnp.bfloat16)
-    lo = (x - hi.astype(jnp.float32)).astype(jnp.bfloat16)
-    return jnp.concatenate([hi, lo], axis=-1)
-
-
-def pack_kernel(x_ref, out_ref):
-    out_ref[...] = split_parts(x_ref[...])
-
-
-def pack(features):
+    hi = x.astype(jnp.bfloat16).astype(jnp.float32)
+    return hi, x - hi
+
+
+TOP = float(8191 << 6)
+
+
+def encode(x):
+    top = jnp.max(jnp.abs(x), axis=(0, 1), keepdims=True)
+    u = jnp.minimum(jnp.abs(x) * jnp.where(top > 0, TOP / top, 0.0), TOP)
+    shift = jnp.zeros(x.shape, jnp.int32)
+    down = jnp.ones(x.shape, jnp.float32)
+    for j in range(1, 7):
+        above = u >= float(4096 << j)
+        shift = jnp.where(above, j, shift)
+        down = jnp.where(above, 0.5 ** j, down)
+    code = shift * 4096 + jnp.floor(u * down + 0.5).astype(jnp.int32)
+    code = jnp.where(x < 0, -code, code)
+    low = jnp.concatenate([code[0:BLK], code[2 * BLK:3 * BLK]], axis=1)
+    high = jnp.concatenate([code[BLK:2 * BLK], code[3 * BLK:]], axis=1)
+    return high * 65536 + low, top * (1.0 / TOP)
+
+
+def decode(code, scale):
+    size = jnp.abs(code)
+    shift = jnp.maximum((size >> 12) - 1, 0)
+    value = (size - (shift << 12)) << shift
+    return jnp.where(code < 0, -value, value).astype(jnp.float32) * scale
+
+
+def pack_kernel(count, x_ref, cols_ref, tiles_ref, out_ref, scale_ref, cols_out, tiles_out):
+    words, scale = encode(x_ref[...].T)
+    out_ref[...] = words
+    scale_ref[...] = jnp.broadcast_to(scale, (1, 2 * BLK))
+    cols_out[...] = jnp.zeros((8, 128), jnp.int32)
+    cols_out[0:4, 0:8] = cols_ref[...]
+    slots = lax.axis_index("col") * 8 + lax.broadcasted_iota(jnp.int32, (8, 4096), 0)
+    for i in range(4):
+        tile = tiles_ref[i].astype(jnp.float32)
+        tiles_out[i] = jnp.where(slots < count[i], tile, 0.0).astype(jnp.bfloat16)
+
+
+def pack(features, adj_values, adj_cols, adj_count):
+    vmem = pl.BlockSpec(memory_space=pltpu.VMEM)
     return pl.pallas_call(
         pack_kernel,
-        out_shape=jax.ShapeDtypeStruct((256, 2 * BLK), jnp.bfloat16),
-    )(features)
+        out_shape=[jax.ShapeDtypeStruct((BLK, 2 * BLK), jnp.int32),
+                   jax.ShapeDtypeStruct((1, 2 * BLK), jnp.float32),
+                   jax.ShapeDtypeStruct((8, 128), jnp.int32),
+                   jax.ShapeDtypeStruct((4, 8, 4096), jnp.bfloat16)],
+        in_specs=[pl.BlockSpec(memory_space=pltpu.SMEM)] + [vmem] * 3,
+        out_specs=[vmem] * 4,
+    )(adj_count, features.T, adj_cols, adj_values)
 
 
 def ring_program():
@@ -67,9 +106,10 @@
 
 def gather_kernel(with_adj, *refs):
     if with_adj:
-        shard, tiles, cols, nodes, tiles_all, cols_all, send, recv, local, adj_send, adj_recv, adj_local = refs
+        (shard, scale, tiles, cols, nodes, scales, tiles_all, cols_all,
+         send, recv, scale_send, scale_recv, local, adj_send, adj_recv, adj_local) = refs
     else:
-        shard, nodes, send, recv, local = refs
+        shard, scale, nodes, scales, send, recv, scale_send, scale_recv, local = refs
     row = lax.axis_index("row")
     col = lax.axis_index("col")
     zh = lax.rem(row, NZ)
@@ -99,11 +139,10 @@
         iy = slice(None) if slab[1] is None else lax.rem(y + slab[1] + NY, NY)
         iz = zh if rel == 0 else 1 - zh
         isub = slice(None) if sub is None else sub
-        return nodes.at[ix, iy, iz, half, isub]
-
-    order = {}
+        return nodes.at[ix, iy, iz, half, isub], scales.at[ix, iy, iz]
+
     flying = {}
-    pending = []
+    riding = {}
 
     def remote(src, dst, sems, k, dev):
         c = pltpu.make_async_remote_copy(
@@ -113,20 +152,27 @@
         return c
 
     mine = nodes.at[x, y, zh]
-    own = pltpu.make_async_copy(shard, mine, local)
-    own.start()
+    mine_scale = scales.at[x, y, zh]
+    own = [pltpu.make_async_copy(shard, mine, local.at[0]),
+           pltpu.make_async_copy(scale, mine_scale, local.at[1])]
+    for c in own:
+        c.start()
     flying["z"] = remote(shard, mine, (send, recv), 0, device(x, y, 1 - zh))
+    riding["z"] = remote(scale, mine_scale, (scale_send, scale_recv), 0, device(x, y, 1 - zh))
     counter = 1
     adj = {}
 
     def issue(sends):
         nonlocal counter
         for key, rel, half, slab, sub, axis, sign in sends:
-            dst = slab_of(rel, half, slab, sub)
-            src = dst
+            dst, dst_scale = slab_of(rel, half, slab, sub)
+            src, src_scale = dst, dst_scale
             if rel == 0 and slab == (0, 0):
-                src = shard.at[half] if sub is None else shard.at[half, sub]
+                src, src_scale = shard.at[half], scale
             flying[key] = remote(src, dst, (send, recv), counter, hop(axis, sign))
+            if half == 0 and sub in (None, 0):
+                riding[key] = remote(src_scale, dst_scale, (scale_send, scale_recv),
+                                     len(riding), hop(axis, sign))
             counter += 1
 
     waited_own = False
@@ -136,9 +182,12 @@
         for key in needs:
             if key not in waited:
                 flying[key].wait_recv()
+                if key in riding:
+                    riding[key].wait_recv()
                 waited.add(key)
         if not waited_own and any(s[3] != (0, 0) for s in sends):
-            own.wait()
+            for c in own:
+                c.wait()
             waited_own = True
         issue(sends)
         if with_adj and not adj_started and slot == 0 and half == 1:
@@ -166,17 +215,21 @@
             c.wait_send()
         for c in adj_own:
             c.wait()
-    for key in flying:
-        flying[key].wait_send()
-
-
-def gather(shard, tiles=None, cols=None, collective_id=0):
+    for copy in list(flying.values()) + list(riding.values()):
+        copy.wait_send()
+
+
+def gather(shard, scale, tiles=None, cols=None, collective_id=0):
     with_adj = tiles is not None
     steps = 1 + sum(len(p[4]) for p in ring_program())
-    out_shape = [jax.ShapeDtypeStruct((NX, NY, NZ, 2, 2, BLK, 2 * BLK), jnp.bfloat16)]
-    args = [shard.reshape(2, 2, BLK, 2 * BLK)]
+    rides = 1 + sum(half == 0 and sub in (None, 0)
+                    for p in ring_program() for _, _, half, _, sub, _, _ in p[4])
+    out_shape = [jax.ShapeDtypeStruct((NX, NY, NZ, 2, 2, 16, 128), jnp.int32),
+                 jax.ShapeDtypeStruct((NX, NY, NZ, 1, 128), jnp.float32)]
+    args = [shard.reshape(2, 2, 16, 128), scale]
     scratch = [pltpu.SemaphoreType.DMA((steps,)), pltpu.SemaphoreType.DMA((steps,)),
-               pltpu.SemaphoreType.DMA]
+               pltpu.SemaphoreType.DMA((rides,)), pltpu.SemaphoreType.DMA((rides,)),
+               pltpu.SemaphoreType.DMA((2,))]
     if with_adj:
         out_shape += [jax.ShapeDtypeStruct((NC,) + tiles.shape, tiles.dtype),
                       jax.ShapeDtypeStruct((NC,) + cols.shape, cols.dtype)]
@@ -193,40 +246,61 @@
     )(*args)
 
 
-def hop_kernel(packed, cols, tiles, nodes, out_ref, *packed_ref):
+def hop_kernel(packed, cols, scales, tiles, words, out_ref, *rest):
+    nodes = rest[-1]
+
+    def unpack(r, _):
+        scale = scales[r, 0, 0]
+        word = words[r]
+        high = (word + 32768) >> 16
+        left = lax.broadcasted_iota(jnp.int32, (BLK, 2 * BLK), 1) < BLK
+        for half, code in ((0, word - (high << 16)), (1, high)):
+            hi, lo = split_parts(decode(code, scale))
+            first = jnp.where(left, hi, pltpu.roll(lo, BLK, 1))
+            second = jnp.where(left, pltpu.roll(hi, BLK, 1), lo)
+            nodes[r * 4 + half] = first.astype(jnp.bfloat16)
+            nodes[r * 4 + half + 2] = second.astype(jnp.bfloat16)
+        return 0
+
+    lax.fori_loop(0, NX * NY * NZ, unpack, 0, unroll=2)
+    totals = []
     for i in range(4):
         acc = jnp.zeros((BLK, 2 * BLK), jnp.float32)
         for j in range(NC):
             picked = jnp.concatenate([nodes[cols[j, i, s]] for s in range(8)], axis=0)
             acc += jnp.dot(tiles[j, i], picked, preferred_element_type=jnp.float32)
-        total = acc[:, :BLK] + acc[:, BLK:]
-        out_ref[pl.ds(i * BLK, BLK), :] = total
-        if packed:
-            packed_ref[0][pl.ds(i * BLK, BLK), :] = split_parts(total)
-
-
-def hop(nodes, tiles, cols, packed):
-    out_shape = [jax.ShapeDtypeStruct((256, BLK), jnp.float32)]
+        totals.append(acc[:, :BLK] + acc[:, BLK:])
+    total = jnp.concatenate(totals, axis=0)
+    out_ref[...] = total.T
     if packed:
-        out_shape.append(jax.ShapeDtypeStruct((256, 2 * BLK), jnp.bfloat16))
-    return pl.pallas_call(
+        words_out, scale = encode(total)
+        rest[0][...] = words_out
+        rest[1][...] = jnp.broadcast_to(scale, (1, 2 * BLK))
+
+
+def hop(words, scales, tiles, cols, packed):
+    smem, vmem = (pl.BlockSpec(memory_space=m) for m in (pltpu.SMEM, pltpu.VMEM))
+    out_shape = [jax.ShapeDtypeStruct((BLK, 256), jnp.float32)]
+    if packed:
+        out_shape += [jax.ShapeDtypeStruct((BLK, 2 * BLK), jnp.int32),
+                      jax.ShapeDtypeStruct((1, 2 * BLK), jnp.float32)]
+    out = pl.pallas_call(
         functools.partial(hop_kernel, packed),
         out_shape=out_shape,
-        in_specs=[pl.BlockSpec(memory_space=pltpu.SMEM)] + [pl.BlockSpec(memory_space=pltpu.VMEM)] * 2,
-        out_specs=[pl.BlockSpec(memory_space=pltpu.VMEM)] * len(out_shape),
-    )(cols, tiles, nodes.reshape(256, BLK, 2 * BLK))
+        in_specs=[smem, smem, vmem, vmem],
+        out_specs=[vmem] * len(out_shape),
+        scratch_shapes=[pltpu.VMEM((256, BLK, 2 * BLK), jnp.bfloat16)],
+    )(cols, scales.reshape(64, 1, 128), tiles, words.reshape(64, BLK, 128))
+    return [out[0].T] + list(out[1:])
 
 
 def local(features, adj_values, adj_cols, adj_count):
-    slots = lax.axis_index("col") * 8 + jnp.arange(8, dtype=jnp.int32)
-    live = slots[None, :, None] < adj_count[:, None, None]
-    tiles = jnp.where(live, adj_values, jnp.zeros_like(adj_values))
+    shard, scale, cols, tiles = pack(features, adj_values, adj_cols, adj_count)
     tiles = tiles.reshape(4, 8, BLK, BLK).transpose(0, 2, 1, 3).reshape(4, BLK, 8 * BLK)
-    cols = jnp.pad(adj_cols, ((0, 4), (0, 120)))
-    nodes, tiles_all, cols_all = gather(pack(features), tiles, cols, collective_id=0)
-    hop_one, shard = hop(nodes, tiles_all, cols_all, True)
-    (second,) = gather(shard, collective_id=1)
-    (hop_two,) = hop(second, tiles_all, cols_all, False)
+    nodes, scales, tiles_all, cols_all = gather(shard, scale, tiles, cols, collective_id=0)
+    hop_one, shard, scale = hop(nodes, scales, tiles_all, cols_all, True)
+    nodes, scales = gather(shard, scale, collective_id=1)
+    (hop_two,) = hop(nodes, scales, tiles_all, cols_all, False)
     return hop_one, hop_two
 
 

time: 134 us -> 120 us (0.90)
  the two profiles are of different devices: /device:TPU:24 before, /device:TPU:64 now
where the time goes in v2:
time: 120 us; the launch traced here: 119 us
  Pallas kernels  116 us (97%)
  local copies, waits for them, and re-layouts  2.84 us (2%)
    pallas_call x2, Pallas kernels, gather(): pl.pallas_call(functools.partial(gather_kernel, with_adj), out_shape=out_...  95.3 us
    pallas_call x2, Pallas kernels, hop(): pl.pallas_call(functools.partial(hop_kernel, packed), out_shape=out_shape...  18.6 us
    reshape x3, local copies, waits for them, and re-layouts, local(): tiles.reshape(4, 8, BLK, BLK).transpose(0, 2, 1, 3).reshape(4, BLK, 8 * BLK)  2.84 us

profile of v2, /device:TPU:64, one launch (start us, length us, event | category | flops | bytes accessed | tf_op | source)
XLA Modules:
  0.0 119.4 jit_solution(6132678938845791963)
XLA Ops:
  0.6 2.1 %shard_map.59 = (s32[64,128]{1,0:T(8,128)}, f32[1,128]{1,0:T(1,128)}, s32[8,128]{1,0:T(8,128)}, bf16[4,8,4096]{2,1,0:T(8,128)(2,1)}) custom-call(s32[4]{0:T(128)} %count.1, f32[64,256]{1,0:T(8,128)} %bitcast.18, s32[4,8]{1,0:T(4,128)} %cols_ref.1, bf16[4,8,4096]{2,1,0:T(8,128)(2,1)} %tiles_ref.1), custom_call_target="tpu_custom_call" | custom-call | tf_op jit(solution)/shard_map/pallas_call | solution.py:61
  2.7 1.5 %reshape.29 = bf16[4,8,64,64]{3,2,1,0:T(8,128)(2,1)S(1)} reshape(bf16[4,8,4096]{2,1,0:T(8,128)(2,1)} %get-tuple-element.17) | data formatting | bytes 524288 | tf_op jit(solution)/shard_map/reshape | solution.py:299
  4.2 0.3 copy.8
  4.6 1.0 reshape.30.refs_2_
  5.6 53.4 %shard_map.60 = (s32[4,8,2,2,2,16,128]{6,5,4,3,2,1,0:T(8,128)}, f32[4,8,2,1,128]{4,3,2,1,0:T(1,128)}, bf16[8,4,64,512]{3,2,1,0:T(8,128)(2,1)}, s32[8,8,128]{2,1,0:T(8,128)}) custom-call(s32[2,2,16,128]{3,2,1,0:T(8,128)} %bitcast.21, f32[1,128]{1,0:T(1,128)} %get-tuple-element.16.refs_1_, bf16[4,64,512]{2,1,0:T(8,128)(2,1)} %reshape.30.refs_2_, ...), custom_call_target="tpu_custom_call" | custom-call | tf_op jit(solution)/shard_map/pallas_call | solution.py:239
  59.0 9.4 %shard_map.61 = (f32[64,256]{1,0:T(8,128)}, s32[64,128]{1,0:T(8,128)}, f32[1,128]{1,0:T(1,128)}) custom-call(s32[8,8,128]{2,1,0:T(8,128)} %get-tuple-element.19.cols, f32[64,1,128]{2,1,0:T(1,128)} %bitcast.19, bf16[8,4,64,512]{3,2,1,0:T(8,128)(2,1)} %get-tuple-element.21.tiles, s32[64,64,128]{2,1,0:T(8,128)} %bitcast.14), custom_call_target="tpu_custom_call" | custom-call | tf_op jit(solution)/shard_map/pallas_call | solution.py:287
  68.4 41.9 %shard_map.62 = (s32[4,8,2,2,2,16,128]{6,5,4,3,2,1,0:T(8,128)}, f32[4,8,2,1,128]{4,3,2,1,0:T(1,128)}) custom-call(s32[2,2,16,128]{3,2,1,0:T(8,128)} %bitcast.22, f32[1,128]{1,0:T(1,128)} %get-tuple-element.25.refs_1_), custom_call_target="tpu_custom_call" | custom-call | tf_op jit(solution)/shard_map/pallas_call | solution.py:239
  110.3 9.1 %shard_map.63 = f32[64,256]{1,0:T(8,128)} custom-call(s32[8,8,128]{2,1,0:T(8,128)} %get-tuple-element.19.cols, f32[64,1,128]{2,1,0:T(1,128)} %bitcast.20, bf16[8,4,64,512]{3,2,1,0:T(8,128)(2,1)} %get-tuple-element.21.tiles, s32[64,64,128]{2,1,0:T(8,128)} %bitcast.15), custom_call_target="tpu_custom_call" | custom-call | tf_op jit(solution)/shard_map/pallas_call | solution.py:287

commit v3 on v2

--- a/solution.py
+++ b/solution.py
@@ -10,6 +10,7 @@
 BLK = 64
 NX, NY, NZ = 4, 8, 2
 NC = 8
+MODES = (("direct", "ring"), ("double", "ring"))
 MESH = pl.DeviceIdType.MESH
 
 
@@ -69,37 +70,40 @@
     )(adj_count, features.T, adj_cols, adj_values)
 
 
-def ring_program():
+def ring_program(modes=MODES, lag=1):
+    size = {"x": NX, "y": NY}
+
+    def moves(n, mode):
+        if mode == "direct":
+            return [[(0, None, 1), (0, None, -1), (0, None, 2)]]
+        if mode == "double":
+            return [[(0, None, 1), (0, None, -1), (0, None, 2), (0, None, -2)],
+                    [(-2, None, 1), (2, None, -1), (-2, 0, 2), (2, 1, -2)]]
+        last = n // 2
+        return [[(-sign * (t - 1), None if t < last else (0 if sign == 1 else 1), sign)
+                 for sign in (1, -1)] for t in range(1, last + 1)]
+
     def stream(rel, half):
-        tag = (rel, half)
-        first, second = ("x", "y") if half == 0 else ("y", "x")
-        size = {"x": NX, "y": NY}
-
-        def phase(axis, whole):
-            n = size[axis]
-            steps = []
-            for t in range(1, n // 2 + 1):
+        steps = []
+        for turn in (0, 1):
+            axis = "xy"[turn ^ half]
+            for t, step in enumerate(moves(size[axis], modes[half][turn])):
                 sends = []
-                for sign in (1, -1):
-                    off = -sign * (t - 1)
+                for off, sub, jump in step:
+                    whole = 0 if turn == 0 else None
                     slab = (off, whole) if axis == "x" else (whole, off)
-                    sub = None if t < n // 2 else (0 if sign == 1 else 1)
-                    sends.append(((tag, axis, t, sign), rel, half, slab, sub, axis, sign))
+                    sends.append(((rel, half, axis, t, jump), rel, half, slab, sub, axis, jump))
                 steps.append(sends)
-            return steps
-
-        return phase(first, 0) + phase(second, None)
+        return steps
 
     program = []
     for rel in (0, 1):
         for half in (0, 1):
             steps = stream(rel, half)
             for t, sends in enumerate(steps):
-                needs = [] if t == 0 else [s[0] for s in steps[t - 1]]
-                if t == 0 and rel == 1:
-                    needs = ["z"]
-                program.append((t + 2 * rel, rel, half, needs, sends))
-            program.append((len(steps) + 2 * rel, rel, half, [s[0] for s in steps[-1]], []))
+                needs = (["z"] if rel == 1 else []) if t == 0 else [s[0] for s in steps[t - 1]]
+                program.append((t + lag * rel, rel, half, needs, sends))
+            program.append((len(steps) + lag * rel, rel, half, [s[0] for s in steps[-1]], []))
     program.sort(key=lambda p: p[0])
     return program
 
@@ -125,7 +129,7 @@
             return device(lax.rem(x + sign + NX, NX), y, zh)
         return device(x, lax.rem(y + sign + NY, NY), zh)
 
-    partners = [hop(a, s) for a in ("x", "y") for s in (1, -1)] + [device(x, y, 1 - zh)]
+    partners = [hop("x", s) for s in (1, -1, 2)] + [hop("y", s) for s in (1, -1, 2, -2)] + [device(x, y, 1 - zh)]
     if with_adj:
         others = [lax.rem(col + j, NC) for j in range(1, NC)]
         partners += [(row, c) for c in others]
@@ -240,7 +244,7 @@
         functools.partial(gather_kernel, with_adj),
         out_shape=out_shape,
         in_specs=[pl.BlockSpec(memory_space=pltpu.VMEM)] * len(args),
-        out_specs=[pl.BlockSpec(memory_space=pl.ANY)] * len(out_shape),
+        out_specs=[pl.BlockSpec(memory_space=pltpu.VMEM)] * len(out_shape),
         scratch_shapes=scratch,
         compiler_params=pltpu.CompilerParams(collective_id=collective_id, has_side_effects=True),
     )(*args)

time: 120 us -> 107 us (0.89)
  the two profiles are of different devices: /device:TPU:64 before, /device:TPU:66 now
where the time goes in v3:
time: 107 us
  Pallas kernels  103 us (96%)
  local copies, waits for them, and re-layouts  2.84 us (3%)
    pallas_call x2, Pallas kernels, gather(): pl.pallas_call(functools.partial(gather_kernel, with_adj), out_shape=out_...  82.7 us
    pallas_call x2, Pallas kernels, hop(): pl.pallas_call(functools.partial(hop_kernel, packed), out_shape=out_shape...  18.6 us
    reshape x3, local copies, waits for them, and re-layouts, local(): tiles.reshape(4, 8, BLK, BLK).transpose(0, 2, 1, 3).reshape(4, BLK, 8 * BLK)  2.84 us

profile of v3, /device:TPU:66, one launch (start us, length us, event | category | flops | bytes accessed | tf_op | source)
XLA Modules:
  0.0 106.8 jit_solution(13912009338305559435)
XLA Ops:
  0.6 2.1 %shard_map.59 = (s32[64,128]{1,0:T(8,128)}, f32[1,128]{1,0:T(1,128)}, s32[8,128]{1,0:T(8,128)}, bf16[4,8,4096]{2,1,0:T(8,128)(2,1)}) custom-call(s32[4]{0:T(128)} %count.1, f32[64,256]{1,0:T(8,128)} %bitcast.18, s32[4,8]{1,0:T(4,128)} %cols_ref.1, bf16[4,8,4096]{2,1,0:T(8,128)(2,1)} %tiles_ref.1), custom_call_target="tpu_custom_call" | custom-call | tf_op jit(solution)/shard_map/pallas_call | solution.py:62
  2.7 1.5 %reshape.29 = bf16[4,8,64,64]{3,2,1,0:T(8,128)(2,1)S(1)} reshape(bf16[4,8,4096]{2,1,0:T(8,128)(2,1)} %get-tuple-element.17) | data formatting | bytes 524288 | tf_op jit(solution)/shard_map/reshape | solution.py:303
  4.2 0.3 copy.8
  4.6 1.0 reshape.30.refs_2_
  5.6 47.8 %shard_map.60 = (s32[4,8,2,2,2,16,128]{6,5,4,3,2,1,0:T(8,128)}, f32[4,8,2,1,128]{4,3,2,1,0:T(1,128)}, bf16[8,4,64,512]{3,2,1,0:T(8,128)(2,1)}, s32[8,8,128]{2,1,0:T(8,128)}) custom-call(s32[2,2,16,128]{3,2,1,0:T(8,128)} %bitcast.21, f32[1,128]{1,0:T(1,128)} %get-tuple-element.16.refs_1_, bf16[4,64,512]{2,1,0:T(8,128)(2,1)} %reshape.30.refs_2_, ...), custom_call_target="tpu_custom_call" | custom-call | tf_op jit(solution)/shard_map/pallas_call | solution.py:243
  53.4 9.4 %shard_map.61 = (f32[64,256]{1,0:T(8,128)}, s32[64,128]{1,0:T(8,128)}, f32[1,128]{1,0:T(1,128)}) custom-call(s32[8,8,128]{2,1,0:T(8,128)} %get-tuple-element.19.cols, f32[64,1,128]{2,1,0:T(1,128)} %bitcast.19, bf16[8,4,64,512]{3,2,1,0:T(8,128)(2,1)} %get-tuple-element.21.tiles, s32[64,64,128]{2,1,0:T(8,128)} %bitcast.14), custom_call_target="tpu_custom_call" | custom-call | tf_op jit(solution)/shard_map/pallas_call | solution.py:291
  62.8 34.9 %shard_map.62 = (s32[4,8,2,2,2,16,128]{6,5,4,3,2,1,0:T(8,128)}, f32[4,8,2,1,128]{4,3,2,1,0:T(1,128)}) custom-call(s32[2,2,16,128]{3,2,1,0:T(8,128)} %bitcast.22, f32[1,128]{1,0:T(1,128)} %get-tuple-element.25.refs_1_), custom_call_target="tpu_custom_call" | custom-call | tf_op jit(solution)/shard_map/pallas_call | solution.py:243
  97.7 9.1 %shard_map.63 = f32[64,256]{1,0:T(8,128)} custom-call(s32[8,8,128]{2,1,0:T(8,128)} %get-tuple-element.19.cols, f32[64,1,128]{2,1,0:T(1,128)} %bitcast.20, bf16[8,4,64,512]{3,2,1,0:T(8,128)(2,1)} %get-tuple-element.21.tiles, s32[64,64,128]{2,1,0:T(8,128)} %bitcast.15), custom_call_target="tpu_custom_call" | custom-call | tf_op jit(solution)/shard_map/pallas_call | solution.py:291

commit v4 on v0

v4 whole, which is shorter than its diff:
```python
import jax
import jax.numpy as jnp
from jax import lax
from jax.experimental import pallas as pl
from jax.experimental.pallas import tpu as pltpu
from jax.sharding import PartitionSpec as P

BLK = 64
NX, NY, NZ = 4, 8, 2
NC = 8
MODES = (("direct", "ring"), ("double", "ring"))
MESH = pl.DeviceIdType.MESH


def split_parts(x):
    hi = x.astype(jnp.bfloat16).astype(jnp.float32)
    return hi, x - hi


TOP = float(8191 << 6)


def encode(x):
    top = jnp.max(jnp.abs(x), axis=(0, 1), keepdims=True)
    u = jnp.minimum(jnp.abs(x) * jnp.where(top > 0, TOP / top, 0.0), TOP)
    shift = jnp.zeros(x.shape, jnp.int32)
    down = jnp.ones(x.shape, jnp.float32)
    for j in range(1, 7):
        above = u >= float(4096 << j)
        shift = jnp.where(above, j, shift)
        down = jnp.where(above, 0.5 ** j, down)
    code = shift * 4096 + jnp.floor(u * down + 0.5).astype(jnp.int32)
    code = jnp.where(x < 0, -code, code)
    low = jnp.concatenate([code[0:BLK], code[2 * BLK:3 * BLK]], axis=1)
    high = jnp.concatenate([code[BLK:2 * BLK], code[3 * BLK:]], axis=1)
    return high * 65536 + low, top * (1.0 / TOP)


def decode(code, scale):
    size = jnp.abs(code)
    shift = jnp.maximum((size >> 12) - 1, 0)
    value = (size - (shift << 12)) << shift
    return jnp.where(code < 0, -value, value).astype(jnp.float32) * scale


def pack_kernel(count, x_ref, cols_ref, tiles_ref, out_ref, scale_ref, cols_out, tiles_out):
    words, scale = encode(x_ref[...].T)
    out_ref[...] = words
    scale_ref[...] = jnp.broadcast_to(scale, (1, 2 * BLK))
    cols_out[...] = jnp.zeros((8, 128), jnp.int32)
    cols_out[0:4, 0:8] = cols_ref[...]
    slots = lax.axis_index("col") * 8 + lax.broadcasted_iota(jnp.int32, (8, 4096), 0)
    for i in range(4):
        tile = tiles_ref[i].astype(jnp.float32)
        tiles_out[i] = jnp.where(slots < count[i], tile, 0.0).astype(jnp.bfloat16)


def pack(features, adj_values, adj_cols, adj_count):
    vmem = pl.BlockSpec(memory_space=pltpu.VMEM)
    return pl.pallas_call(
        pack_kernel,
        out_shape=[jax.ShapeDtypeStruct((BLK, 2 * BLK), jnp.int32),
                   jax.ShapeDtypeStruct((1, 2 * BLK), jnp.float32),
                   jax.ShapeDtypeStruct((8, 128), jnp.int32),
                   jax.ShapeDtypeStruct((4, 8, 4096), jnp.bfloat16)],
        in_specs=[pl.BlockSpec(memory_space=pltpu.SMEM)] + [vmem] * 3,
        out_specs=[vmem] * 4,
    )(adj_count, features.T, adj_cols, adj_values)


def ring_program(modes=MODES, lag=1):
    size = {"x": NX, "y": NY}

    def moves(n, mode):
        if mode == "direct":
            return [[(0, None, 1), (0, None, -1), (0, None, 2)]]
        if mode == "double":
            return [[(0, None, 1), (0, None, -1), (0, None, 2), (0, None, -2)],
                    [(-2, None, 1), (2, None, -1), (-2, 0, 2), (2, 1, -2)]]
        last = n // 2
        return [[(-sign * (t - 1), None if t < last else (0 if sign == 1 else 1), sign)
                 for sign in (1, -1)] for t in range(1, last + 1)]

    def stream(rel, half):
        steps = []
        for turn in (0, 1):
            axis = "xy"[turn ^ half]
            for t, step in enumerate(moves(size[axis], modes[half][turn])):
                sends = []
                for off, sub, jump in step:
                    whole = 0 if turn == 0 else None
                    slab = (off, whole) if axis == "x" else (whole, off)
                    sends.append(((rel, half, axis, t, jump), rel, half, slab, sub, axis, jump))
                steps.append(sends)
        return steps

    program = []
    for rel in (0, 1):
        for half in (0, 1):
            steps = stream(rel, half)
            for t, sends in enumerate(steps):
                needs = (["z"] if rel == 1 else []) if t == 0 else [s[0] for s in steps[t - 1]]
                program.append((t + lag * rel, rel, half, needs, sends))
            program.append((len(steps) + lag * rel, rel, half, [s[0] for s in steps[-1]], []))
    program.sort(key=lambda p: p[0])
    return program


def unpack(words, scales, nodes, zh):
    left = lax.broadcasted_iota(jnp.int32, (BLK, 2 * BLK), 1) < BLK

    def one(q, _):
        x, y = q // NY, lax.rem(q, NY)
        r = q * NZ + zh
        scale = scales[x, y, zh]
        word = words[x, y, zh].reshape(BLK, 2 * BLK)
        high = (word + 32768) >> 16
        for half, code in ((0, word - (high << 16)), (1, high)):
            hi, lo = split_parts(decode(code, scale))
            first = jnp.where(left, hi, pltpu.roll(lo, BLK, 1))
            second = jnp.where(left, pltpu.roll(hi, BLK, 1), lo)
            nodes[r * 4 + half] = first.astype(jnp.bfloat16)
            nodes[r * 4 + half + 2] = second.astype(jnp.bfloat16)
        return 0

    lax.fori_loop(0, NX * NY, one, 0, unroll=2)


def multiply(cols, tiles, nodes):
    totals = []
    for i in range(4):
        acc = jnp.zeros((BLK, 2 * BLK), jnp.float32)
        for j in range(NC):
            picked = jnp.concatenate([nodes[cols[j, i, s]] for s in range(8)], axis=0)
            acc += jnp.dot(tiles[j, i], picked, preferred_element_type=jnp.float32)
        totals.append(acc[:, :BLK] + acc[:, BLK:])
    return jnp.concatenate(totals, axis=0)


def kernel(shard, scale, tiles, cols, out_one, out_two, words_one, words_two, scales_one,
           scales_two, tiles_all, cols_all, cols_smem, nodes, shard_two, scale_two, send, recv,
           scale_send, scale_recv, local, adj_send, adj_recv, adj_local):
    row = lax.axis_index("row")
    col = lax.axis_index("col")
    zh = lax.rem(row, NZ)
    y = lax.rem(row // NZ, NY)
    x = row // (NZ * NY)
    zl, core = col // 2, lax.rem(col, 2)

    def device(px, py, pz):
        return ((px * NY + py) * NZ + pz, col)

    def hop(axis, jump):
        if axis == "x":
            return device(lax.rem(x + jump + NX, NX), y, zh)
        return device(x, lax.rem(y + jump + NY, NY), zh)

    others = [lax.rem(col + j, NC) for j in range(1, NC)]
    partners = [hop("x", j) for j in (1, -1, 2)] + [hop("y", j) for j in (1, -1, 2, -2)]
    partners += [device(x, y, 1 - zh)] + [(row, c) for c in others]
    barrier = pltpu.get_barrier_semaphore()
    for p in partners:
        pl.semaphore_signal(barrier, inc=1, device_id=p, device_id_type=MESH)
    pl.semaphore_wait(barrier, len(partners))

    def remote(src, dst, sems, k, dev):
        c = pltpu.make_async_remote_copy(
            src_ref=src, dst_ref=dst, send_sem=sems[0].at[k], recv_sem=sems[1].at[k],
            device_id=dev, device_id_type=MESH)
        c.start()
        return c

    def gather(g, shard, scale, words, scales, after_start):
        main = (send.at[g], recv.at[g])
        side = (scale_send.at[g], scale_recv.at[g])

        def slab_of(rel, half, slab, sub):
            ix = slice(None) if slab[0] is None else lax.rem(x + slab[0] + NX, NX)
            iy = slice(None) if slab[1] is None else lax.rem(y + slab[1] + NY, NY)
            iz = zh if rel == 0 else 1 - zh
            isub = slice(None) if sub is None else sub
            return words.at[ix, iy, iz, half, isub], scales.at[ix, iy, iz]

        mine, mine_scale = words.at[x, y, zh], scales.at[x, y, zh]
        twin = device(x, y, 1 - zh)
        flying = {"z": remote(shard, mine, main, 0, twin)}
        riding = {"z": remote(scale, mine_scale, side, 0, twin)}
        own = [pltpu.make_async_copy(shard, mine, local.at[g, 0]),
               pltpu.make_async_copy(scale, mine_scale, local.at[g, 1])]
        for c in own:
            c.start()
        waited, started, waited_own, decoded = set(), False, False, False
        program = ring_program()
        for slot, rel, half, needs, sends in program:
            if slot > 0 and not started:
                started = True
                after_start()
            if slot == program[-1][0] and not decoded:
                decoded = True
                unpack(words, scales, nodes, zh)
            for key in needs:
                if key not in waited:
                    flying[key].wait_recv()
                    if key in riding:
                        riding[key].wait_recv()
                    waited.add(key)
            if not waited_own and any(s[3] != (0, 0) for s in sends):
                for c in own:
                    c.wait()
                waited_own = True
            for key, rel, half, slab, sub, axis, jump in sends:
                dst, dst_scale = slab_of(rel, half, slab, sub)
                src, src_scale = dst, dst_scale
                if rel == 0 and slab == (0, 0):
                    src, src_scale = shard.at[half], scale
                flying[key] = remote(src, dst, main, len(flying), hop(axis, jump))
                if half == 0 and sub in (None, 0):
                    riding[key] = remote(src_scale, dst_scale, side, len(riding), hop(axis, jump))
        unpack(words, scales, nodes, 1 - zh)
        return list(flying.values()) + list(riding.values())

    adj = []

    def start_adj():
        sems = (adj_send, adj_recv)
        adj.extend([
            [remote(tiles, tiles_all.at[col], sems, j - 1,
                    (row, lax.rem(zl + j, 4) * 2 + core)) for j in range(1, 4)],
            [remote(tiles, tiles_all.at[col], sems, 3, (row, zl * 2 + 1 - core))],
            [remote(cols, cols_all.at[col], sems, 7 + j, (row, others[j]))
             for j in range(NC - 1)],
            [pltpu.make_async_copy(tiles, tiles_all.at[col], adj_local.at[0]),
             pltpu.make_async_copy(cols, cols_all.at[col], adj_local.at[1])]])
        for c in adj[3]:
            c.start()

    sent = gather(0, shard, scale, words_one, scales_one, start_adj)
    across, twin, ids, adj_own = adj
    for j in range(1, 4):
        across[j - 1].wait_recv()
        piece = tiles_all.at[lax.rem(zl + 4 - j, 4) * 2 + core]
        twin.append(remote(piece, piece, (adj_send, adj_recv), 3 + j, (row, zl * 2 + 1 - core)))
    for c in ids:
        c.wait_recv()
    for c in adj_own:
        c.wait()
    to_smem = pltpu.make_async_copy(cols_all, cols_smem, adj_local.at[2])
    to_smem.start()
    to_smem.wait()
    for c in twin:
        c.wait_recv()

    total = multiply(cols_smem, tiles_all, nodes)
    codes, top = encode(total)
    shard_two[...] = codes.reshape(2, 2, 16, 2 * BLK)
    scale_two[...] = jnp.broadcast_to(top, (1, 2 * BLK))
    out_one[...] = total.T
    sent += gather(1, shard_two, scale_two, words_two, scales_two, lambda: None)
    out_two[...] = multiply(cols_smem, tiles_all, nodes).T
    for c in sent + across + twin + ids:
        c.wait_send()


def two_hops(shard, scale, tiles, cols):
    program = ring_program()
    sends = [s for p in program for s in p[4]]
    steps = 1 + len(sends)
    rides = 1 + sum(s[2] == 0 and s[4] in (None, 0) for s in sends)
    vmem = pl.BlockSpec(memory_space=pltpu.VMEM)
    dma = pltpu.SemaphoreType.DMA
    words = pltpu.VMEM((NX, NY, NZ, 2, 2, 16, 128), jnp.int32)
    scales = pltpu.VMEM((NX, NY, NZ, 1, 128), jnp.float32)
    one, two = pl.pallas_call(
        kernel,
        out_shape=[jax.ShapeDtypeStruct((BLK, 256), jnp.float32)] * 2,
        in_specs=[vmem] * 4,
        out_specs=[vmem] * 2,
        scratch_shapes=[words, words, scales, scales,
                        pltpu.VMEM((NC,) + tiles.shape, tiles.dtype),
                        pltpu.VMEM((NC,) + cols.shape, cols.dtype),
                        pltpu.SMEM((NC,) + cols.shape, cols.dtype),
                        pltpu.VMEM((256, BLK, 2 * BLK), jnp.bfloat16),
                        pltpu.VMEM((2, 2, 16, 128), jnp.int32),
                        pltpu.VMEM((1, 128), jnp.float32),
                        dma((2, steps)), dma((2, steps)), dma((2, rides)), dma((2, rides)),
                        dma((2, 2)), dma((14,)), dma((14,)), dma((3,))],
        compiler_params=pltpu.CompilerParams(collective_id=0, has_side_effects=True),
    )(shard.reshape(2, 2, 16, 128), scale, tiles, cols)
    return one.T, two.T


def local(features, adj_values, adj_cols, adj_count):
    shard, scale, cols, tiles = pack(features, adj_values, adj_cols, adj_count)
    tiles = tiles.reshape(4, 8, BLK, BLK).transpose(0, 2, 1, 3).reshape(4, BLK, 8 * BLK)
    return two_hops(shard, scale, tiles, cols)


def solution(mesh):
    in_specs = (P("row", "col"), P("row", "col", None), P("row", "col"), P("row"))
    out_specs = (P("row", "col"), P("row", "col"))
    return jax.shard_map(local, mesh=mesh, in_specs=in_specs, out_specs=out_specs, check_vma=False)
```

time: 468 us -> 91.9 us (0.20)
  the two profiles are of different devices: /device:TPU:6 before, /device:TPU:64 now
where the time goes in v4:
time: 91.9 us; the launch traced here: 91.6 us
  Pallas kernels  86 us (94%)
  local copies, waits for them, and re-layouts  4.96 us (5%)
    pallas_call x1, Pallas kernels, two_hops(): pl.pallas_call(kernel, out_shape=[jax.ShapeDtypeStruct((BLK, 256), jnp.fl...  83.9 us
    reshape x3, local copies, waits for them, and re-layouts, local(): tiles.reshape(4, 8, BLK, BLK).transpose(0, 2, 1, 3).reshape(4, BLK, 8 * BLK)  2.83 us
    unnamed x4, local copies, waits for them, and re-layouts  2.14 us
    pallas_call x1, Pallas kernels, pack(): pl.pallas_call(pack_kernel, out_shape=[jax.ShapeDtypeStruct((BLK, 2 * BLK...  2.12 us

profile of v4, /device:TPU:64, one launch (start us, length us, event | category | flops | bytes accessed | tf_op | source)
XLA Modules:
  0.0 91.6 jit_solution(13380757694683622130)
XLA Ops:
  0.6 2.1 %shard_map.59 = (s32[64,128]{1,0:T(8,128)}, f32[1,128]{1,0:T(1,128)}, s32[8,128]{1,0:T(8,128)}, bf16[4,8,4096]{2,1,0:T(8,128)(2,1)}) custom-call(s32[4]{0:T(128)} %count.1, f32[64,256]{1,0:T(8,128)} %bitcast.10, s32[4,8]{1,0:T(4,128)} %cols_ref.1, bf16[4,8,4096]{2,1,0:T(8,128)(2,1)} %tiles_ref.1), custom_call_target="tpu_custom_call" | custom-call | tf_op jit(solution)/shard_map/pallas_call | solution.py:60
  2.7 1.5 %reshape.14 = bf16[4,8,64,64]{3,2,1,0:T(8,128)(2,1)S(1)} reshape(bf16[4,8,4096]{2,1,0:T(8,128)(2,1)} %get-tuple-element.10) | data formatting | bytes 524288 | tf_op jit(solution)/shard_map/reshape | solution.py:294
  4.2 0.3 copy.8
  4.6 1.0 %reshape.15.tiles = bf16[4,64,512]{2,1,0:T(8,128)(2,1)} reshape(bf16[4,64,8,64]{3,2,1,0:T(8,128)(2,1)S(1)} %bitcast.9) | data formatting | bytes 524288 | tf_op jit(solution)/shard_map/reshape | solution.py:294
  5.6 83.9 %shard_map.60 = (f32[64,256]{1,0:T(8,128)}, f32[64,256]{1,0:T(8,128)}) custom-call(s32[2,2,16,128]{3,2,1,0:T(8,128)} %bitcast.13, f32[1,128]{1,0:T(1,128)} %get-tuple-element.9.scale, bf16[4,64,512]{2,1,0:T(8,128)(2,1)} %reshape.15.tiles, s32[8,128]{1,0:T(8,128)} %get-tuple-element.11.cols), custom_call_target="tpu_custom_call" | custom-call | tf_op jit(solution)/shard_map/pallas_call | solution.py:273
  89.5 0.0 copy-start
  89.5 1.5 %copy.11 = f32[256,64]{0,1:T(8,128)} copy(f32[256,64]{0,1:T(8,128)} %bitcast.12) | data formatting | bytes 131072
  91.0 0.0 copy-done
  91.0 0.6 copy.12
Async XLA Ops:
  89.5 1.5 %copy-start = (f32[64,256]{1,0:T(8,128)S(1)}, f32[64,256]{1,0:T(8,128)}, u32[]{:S(2)}) copy-start(f32[64,256]{1,0:T(8,128)} %get-tuple-element.13) | copy-start | bytes 196612

commit v5 on v4

--- a/solution.py
+++ b/solution.py
@@ -126,15 +126,19 @@
     lax.fori_loop(0, NX * NY, one, 0, unroll=2)
 
 
-def multiply(cols, tiles, nodes):
-    totals = []
+def multiply(cols, tiles, nodes, parts, accs):
+    out = []
     for i in range(4):
-        acc = jnp.zeros((BLK, 2 * BLK), jnp.float32)
-        for j in range(NC):
+        acc = accs[i]
+        for j in parts:
             picked = jnp.concatenate([nodes[cols[j, i, s]] for s in range(8)], axis=0)
             acc += jnp.dot(tiles[j, i], picked, preferred_element_type=jnp.float32)
-        totals.append(acc[:, :BLK] + acc[:, BLK:])
-    return jnp.concatenate(totals, axis=0)
+        out.append(acc)
+    return out
+
+
+def join(accs):
+    return jnp.concatenate([acc[:, :BLK] + acc[:, BLK:] for acc in accs], axis=0)
 
 
 def kernel(shard, scale, tiles, cols, out_one, out_two, words_one, words_two, scales_one,
@@ -247,16 +251,19 @@
     to_smem = pltpu.make_async_copy(cols_all, cols_smem, adj_local.at[2])
     to_smem.start()
     to_smem.wait()
+    same = [z * 2 + core for z in range(NC // 2)]
+    other = [z * 2 + 1 - core for z in range(NC // 2)]
+    zero = [jnp.zeros((BLK, 2 * BLK), jnp.float32)] * 4
+    accs = multiply(cols_smem, tiles_all, nodes, same, zero)
     for c in twin:
         c.wait_recv()
-
-    total = multiply(cols_smem, tiles_all, nodes)
+    total = join(multiply(cols_smem, tiles_all, nodes, other, accs))
     codes, top = encode(total)
     shard_two[...] = codes.reshape(2, 2, 16, 2 * BLK)
     scale_two[...] = jnp.broadcast_to(top, (1, 2 * BLK))
     out_one[...] = total.T
     sent += gather(1, shard_two, scale_two, words_two, scales_two, lambda: None)
-    out_two[...] = multiply(cols_smem, tiles_all, nodes).T
+    out_two[...] = join(multiply(cols_smem, tiles_all, nodes, same + other, zero)).T
     for c in sent + across + twin + ids:
         c.wait_send()
 

time: 91.9 us -> 92.2 us (level)
  no operation moved by 1% of the time
where the time goes in v5:
time: 92.2 us; the launch traced here: 92 us
  Pallas kernels  86.3 us (94%)
  local copies, waits for them, and re-layouts  4.96 us (5%)
    pallas_call x1, Pallas kernels, two_hops(): pl.pallas_call(kernel, out_shape=[jax.ShapeDtypeStruct((BLK, 256), jnp.fl...  84.2 us
    reshape x3, local copies, waits for them, and re-layouts, local(): tiles.reshape(4, 8, BLK, BLK).transpose(0, 2, 1, 3).reshape(4, BLK, 8 * BLK)  2.83 us
    unnamed x4, local copies, waits for them, and re-layouts  2.14 us
    pallas_call x1, Pallas kernels, pack(): pl.pallas_call(pack_kernel, out_shape=[jax.ShapeDtypeStruct((BLK, 2 * BLK...  2.12 us

profile of v5, /device:TPU:64, one launch (start us, length us, event | category | flops | bytes accessed | tf_op | source)
XLA Modules:
  0.0 92.0 jit_solution(18096390377855964645)
XLA Ops:
  0.6 2.1 %shard_map.59 = (s32[64,128]{1,0:T(8,128)}, f32[1,128]{1,0:T(1,128)}, s32[8,128]{1,0:T(8,128)}, bf16[4,8,4096]{2,1,0:T(8,128)(2,1)}) custom-call(s32[4]{0:T(128)} %count.1, f32[64,256]{1,0:T(8,128)} %bitcast.10, s32[4,8]{1,0:T(4,128)} %cols_ref.1, bf16[4,8,4096]{2,1,0:T(8,128)(2,1)} %tiles_ref.1), custom_call_target="tpu_custom_call" | custom-call | tf_op jit(solution)/shard_map/pallas_call | solution.py:60
  2.7 1.5 %reshape.14 = bf16[4,8,64,64]{3,2,1,0:T(8,128)(2,1)S(1)} reshape(bf16[4,8,4096]{2,1,0:T(8,128)(2,1)} %get-tuple-element.10) | data formatting | bytes 524288 | tf_op jit(solution)/shard_map/reshape | solution.py:301
  4.2 0.3 copy.8
  4.6 1.0 %reshape.15.tiles = bf16[4,64,512]{2,1,0:T(8,128)(2,1)} reshape(bf16[4,64,8,64]{3,2,1,0:T(8,128)(2,1)S(1)} %bitcast.9) | data formatting | bytes 524288 | tf_op jit(solution)/shard_map/reshape | solution.py:301
  5.6 84.2 %shard_map.60 = (f32[64,256]{1,0:T(8,128)}, f32[64,256]{1,0:T(8,128)}) custom-call(s32[2,2,16,128]{3,2,1,0:T(8,128)} %bitcast.13, f32[1,128]{1,0:T(1,128)} %get-tuple-element.9.scale, bf16[4,64,512]{2,1,0:T(8,128)(2,1)} %reshape.15.tiles, s32[8,128]{1,0:T(8,128)} %get-tuple-element.11.cols), custom_call_target="tpu_custom_call" | custom-call | tf_op jit(solution)/shard_map/pallas_call | solution.py:280
  89.8 0.0 copy-start
  89.8 1.5 %copy.11 = f32[256,64]{0,1:T(8,128)} copy(f32[256,64]{0,1:T(8,128)} %bitcast.12) | data formatting | bytes 131072
  91.3 0.0 copy-done
  91.3 0.6 copy.12
Async XLA Ops:
  89.8 1.5 %copy-start = (f32[64,256]{1,0:T(8,128)S(1)}, f32[64,256]{1,0:T(8,128)}, u32[]{:S(2)}) copy-start(f32[64,256]{1,0:T(8,128)} %get-tuple-element.13) | copy-start | bytes 196612
